TPU v7x, 32 devices: a whole 2x2x4 slice. The times are simulated.
32 devices in a mesh: group: 2 (over x), tm: 16 (over z, y, core).
Axes of the slice: x: 2, y: 2, z: 4, core: 2. Of those that a mesh axis runs over, the one named last changes fastest.
Arguments:
- state: bfloat16 [32, 512, 512], P(('group', 'tm')), parts along dimension 0, may hold values from -6 to 6
- noise: bfloat16 [32, 512, 512], P(('group', 'tm')), parts along dimension 0, may hold values from -6 to 6
- gain_first: float32 [512], replicated, may hold values from 0.1 to 1.9
- gain_second: float32 [512], replicated, may hold values from 0.1 to 1.9
- self_query: bfloat16 [512, 512], replicated, may hold values from -16 to 16, as said below
- self_key: bfloat16 [512, 512], replicated, may hold values from -8 to 8, as said below
- self_value: bfloat16 [512, 512], replicated, may hold values from -0.25 to 0.25
- self_out: bfloat16 [512, 512], replicated, may hold values from -0.25 to 0.25
- cross_query: bfloat16 [512, 512], replicated, may hold values from -16 to 16, as said below
- cross_key: bfloat16 [512, 512], replicated, may hold values from -8 to 8, as said below
- cross_value: bfloat16 [512, 512], replicated, may hold values from -0.25 to 0.25
- cross_out: bfloat16 [512, 512], replicated, may hold values from -0.25 to 0.25
- obs_operator: bfloat16 [512, 128], replicated, may hold values from -0.25 to 0.25
- obs_owner: int32 [8192, 1], P(('group', 'tm')), parts along dimension 0, may hold values from 0 to 15; in each aligned block of 256 rows (0 to 255, 256 to 511, ...) at most 16 rows name the same one
- obs_row: int32 [8192], P(('group', 'tm')), parts along dimension 0, may hold values from 0 to 511
- obs_value: bfloat16 [8192, 128], P(('group', 'tm')), parts along dimension 0, may hold values from -6 to 6
Outputs:
- drift: bfloat16 [32, 512, 512], P(('group', 'tm')), parts along dimension 0
- updated: bfloat16 [32, 512, 512], P(('group', 'tm')), parts along dimension 0
There are 2 independent parts, one for each index of `group`. A program takes and returns all parts, laid end to end along the dimension named above; an argument that names none is the same for every part. Nothing has to cross between parts.
Inputs may be any that keep to these rules, and one draw needn't show every extreme that they name: `obs_owner`: among the 256 observations held by one index of tm, at most 16 refer to any one state, and some state receives exactly 16 of them. `self_query`: a query projection. `self_key`: a key projection. `cross_query`: a query projection. `cross_key`: a key projection.
All inputs are finite; a program needn't handle non-finite values.
Results may differ from a plain program's by a relative error of at most 0.014.
The roundings to bfloat16 on the way count: a program that leaves them out, or rounds other values in their place, can miss the bound.
Values may be sent and summed in bfloat16 or wider, within the bound.
A program may use at most 128 MiB of HBM per device.

v0:
```python
import math

import jax
import jax.numpy as jnp
from jax import lax
from jax.sharding import PartitionSpec as P

D = 512
HEADS = 16
OW = 128
CAP = 16


step_size = 0.1
inv_var = 2.0


def shifted(array, axis, by):
    devices = lax.axis_size(axis)
    pairs = [(i, i + by) for i in range(devices) if 0 <= i + by < devices]
    return lax.ppermute(array, axis, pairs)


def rms_norm(vector, gain_vector):
    vector = vector.astype(jnp.float32)
    return (
        vector * lax.rsqrt(jnp.mean(vector * vector, axis=-1, keepdims=True) + 1e-05) * gain_vector
    )


def linear(array, matrix):
    return jnp.dot(array, matrix, preferred_element_type=jnp.float32)


def attend(query, key_rows, value_rows, allowed):
    head_size = D // HEADS
    qb = query.reshape(query.shape[0], HEADS, head_size)
    kb = key_rows.reshape(key_rows.shape[0], HEADS, head_size)
    vb = value_rows.reshape(value_rows.shape[0], HEADS, head_size)
    scores = jnp.einsum("qhd,khd->hqk", qb, kb, preferred_element_type=jnp.float32) * head_size ** (
        -0.5
    )
    scores = jnp.where(allowed[None, None, :], scores, jnp.float32(-1e30))
    largest = jnp.max(scores, axis=-1, keepdims=True)
    exponent = jnp.exp(scores - largest)
    weights = (exponent / jnp.sum(exponent, axis=-1, keepdims=True)).astype(jnp.bfloat16)
    result = jnp.einsum("hqk,khd->qhd", weights, vb, preferred_element_type=jnp.float32)
    return result.reshape(query.shape[0], D).astype(jnp.bfloat16)


def per_device(
    state,
    noise,
    gain_first,
    gain_second,
    self_query,
    self_key,
    self_value,
    self_out,
    cross_query,
    cross_key,
    cross_value,
    cross_out,
    obs_operator,
    obs_owner,
    obs_row,
    obs_value,
):
    tokens = state[0]
    token_count = tokens.shape[0]
    normed = rms_norm(tokens, gain_first).astype(jnp.bfloat16)
    queries = linear(normed, self_query).astype(jnp.bfloat16)
    keys_self = linear(normed, self_key).astype(jnp.bfloat16)
    values_self = linear(normed, self_value).astype(jnp.bfloat16)
    attended = attend(queries, keys_self, values_self, jnp.ones((token_count,), bool))
    middle = (tokens.astype(jnp.float32) + linear(attended, self_out)).astype(jnp.bfloat16)
    lifted = rms_norm(middle, gain_second).astype(jnp.bfloat16)
    cross_q = linear(lifted, cross_query).astype(jnp.bfloat16)
    position = lax.axis_index("tm")
    states = lax.axis_size("tm")
    before_rows = shifted(normed, "tm", 1)
    after_rows = shifted(normed, "tm", -1)
    neighbours = jnp.concatenate([before_rows, after_rows])
    near_keys = linear(neighbours, cross_key).astype(jnp.bfloat16)
    near_values = linear(neighbours, cross_value).astype(jnp.bfloat16)
    allowed = jnp.concatenate(
        [jnp.full((token_count,), position > 0), jnp.full((token_count,), position < states - 1)]
    )
    crossed = attend(cross_q, near_keys, near_values, allowed)
    score = middle.astype(jnp.float32) + linear(crossed, cross_out)
    owners = obs_owner[:, 0]
    onehot = (owners[:, None] == jnp.arange(states, dtype=jnp.int32)[None, :]).astype(jnp.int32)
    slot_number = jnp.sum(jnp.cumsum(onehot, axis=0) * onehot, axis=1) - 1
    destination = owners * CAP + slot_number
    send_value = (
        jnp.zeros((states * CAP, OW), jnp.bfloat16)
        .at[destination]
        .set(obs_value)
        .reshape(states, CAP, OW)
    )
    send_row = (
        jnp.full((states * CAP,), token_count, jnp.int32)
        .at[destination]
        .set(obs_row)
        .reshape(states, CAP)
    )
    values_in = lax.all_to_all(send_value, "tm", split_axis=0, concat_axis=0, tiled=True)
    row_index = lax.all_to_all(send_row, "tm", split_axis=0, concat_axis=0, tiled=True)
    filled = row_index < token_count
    picked = jnp.take(tokens, jnp.minimum(row_index, token_count - 1), axis=0)
    predicted = jnp.einsum("ncd,do->nco", picked, obs_operator, preferred_element_type=jnp.float32)
    misfit = inv_var * (values_in.astype(jnp.float32) - predicted)
    misfit = jnp.where(filled[:, :, None], misfit, jnp.float32(0.0))
    misfit, row_index = (misfit, row_index)
    token_misfit = (
        jnp.zeros((token_count, OW), jnp.float32)
        .at[row_index.reshape(-1)]
        .add(misfit.reshape(-1, OW), mode="drop")
        .astype(jnp.bfloat16)
    )
    gradient = jnp.einsum(
        "to,do->td", token_misfit, obs_operator, preferred_element_type=jnp.float32
    )
    combined = score + gradient
    drift = combined.astype(jnp.bfloat16)
    updated = (
        tokens.astype(jnp.float32)
        + step_size * combined
        + math.sqrt(2.0 * step_size) * noise[0].astype(jnp.float32)
    ).astype(jnp.bfloat16)
    return (drift[None], updated[None])


def solution(mesh):
    return jax.shard_map(
        per_device,
        mesh=mesh,
        in_specs=(
            P(("group", "tm"), None, None),
            P(("group", "tm"), None, None),
            P(),
            P(),
            P(),
            P(),
            P(),
            P(),
            P(),
            P(),
            P(),
            P(),
            P(),
            P(("group", "tm"), None),
            P(("group", "tm")),
            P(("group", "tm"), None),
        ),
        out_specs=(P(("group", "tm"), None, None), P(("group", "tm"), None, None)),
        check_vma=False,
    )
```

profile of v0, /device:TPU:0, one launch (start us, length us, event | category | flops | bytes accessed | tf_op | source)
XLA Modules:
  0.0 103.4 jit_solution(17005525207924818529)
XLA Ops:
  0.6 0.0 copy-start
  0.6 1.3 %copy.44 = bf16[1,512,512]{1,2,0:T(8,128)(2,1)S(1)} copy(bf16[1,512,512]{2,1,0:T(8,128)(2,1)} %param.16) | data formatting | bytes 1048576 | tf_op args[0]
  2.0 0.2 fusion.22
  2.1 0.8 fusion.24
  3.0 3.2 %collective-permute-start = (bf16[512,512]{0,1:T(8,128)(2,1)S(1)}, bf16[512,512]{0,1:T(8,128)(2,1)}, u32[]{:S(2)}, u32[]{:S(2)}) collective-permute-start(bf16[512,512]{0,1:T(8,128)(2,1)S(1)} %fusion.24), channel_id=1, source_target_pairs={{0,1},{1,2},{2,3},{3,4},{4,5},{5,6},{6,7},{7,8},{8,9},{9,10},{10,1... | collective-permute-start | bytes 1572872 | tf_op jit(solution)/shard_map/ppermute | solution.py:21
  6.2 1.3 %collective-permute-start.1 = (bf16[512,512]{0,1:T(8,128)(2,1)S(1)}, bf16[512,512]{0,1:T(8,128)(2,1)}, u32[]{:S(2)}, u32[]{:S(2)}) collective-permute-start(bf16[512,512]{0,1:T(8,128)(2,1)S(1)} %fusion.24), channel_id=1, source_target_pairs={{1,0},{2,1},{3,2},{4,3},{5,4},{6,5},{7,6},{8,7},{9,8},{10,9},{11,1... | collective-permute-start | bytes 1572872 | tf_op jit(solution)/shard_map/ppermute | solution.py:21
  7.4 0.7 fusion.42
  8.1 0.6 reduce-window.6
  8.7 0.2 slice_reduce_fusion
  8.9 0.8 fusion.41
  9.7 0.7 compare_select_fusion.3
  10.4 1.6 %scatter_custom_fusion = s32[256]{0:T(256)S(1)} fusion(s32[256]{0:T(256)S(1)} %bitcast.97, s32[256]{0:T(256)} %param.30, s32[]{:T(128)} %constant.28.clone.1), kind=kCustom, calls=%fused_computation.84 | custom fusion | bytes 1536 | tf_op jit(solution)/shard_map/scatter | solution.py:104
  11.9 0.7 all_to_all.9
  12.6 8.5 %all-to-all-start = ((s32[16,1,16]{2,1,0:T(1,128)}), s32[16,1,16]{2,1,0:T(1,128)S(1)}, u32[]{:S(2)}, u32[]{:S(2)}) async-start(s32[16,1,16]{2,1,0:T(1,128)} %all_to_all.9), calls=%async_computation | async-start | bytes 16384 | tf_op jit(solution)/shard_map/all_to_all | solution.py:108
  21.2 1.5 %convolution_convert_fusion.4 = bf16[512,512]{0,1:T(8,128)(2,1)S(1)} fusion(bf16[512,512]{0,1:T(8,128)(2,1)S(1)} %fusion.24, bf16[512,512]{1,0:T(8,128)(2,1)} %param.20), kind=kOutput, calls=%fused_computation.33 | convolution fusion | flops 268697600 | bytes 1572864 | tf_op jit(solution)/shard_map/dot_general | solution.py:32
  22.7 1.5 %convolution_convert_fusion.3 = bf16[512,512]{0,1:T(8,128)(2,1)S(1)} fusion(bf16[512,512]{0,1:T(8,128)(2,1)S(1)} %fusion.24, bf16[512,512]{1,0:T(8,128)(2,1)} %param.21), kind=kOutput, calls=%fused_computation.32 | convolution fusion | flops 268697600 | bytes 1572864 | tf_op jit(solution)/shard_map/dot_general | solution.py:32
  24.2 1.5 %convolution_convert_fusion.5 = bf16[512,512]{0,1:T(8,128)(2,1)S(1)} fusion(bf16[512,512]{0,1:T(8,128)(2,1)S(1)} %fusion.24, bf16[512,512]{1,0:T(8,128)(2,1)} %param.22), kind=kOutput, calls=%fused_computation.34 | convolution fusion | flops 268697600 | bytes 1572864 | tf_op jit(solution)/shard_map/dot_general | solution.py:32
  25.8 8.8 %fusion.51 = (f32[16,512]{1,0:T(8,128)S(1)}, f32[16,512,512]{1,2,0:T(8,128)}) fusion(bf16[512,16,32]{0,2,1:T(8,128)(2,1)S(1)} %bitcast.87, bf16[512,16,32]{0,2,1:T(8,128)(2,1)S(1)} %bitcast.88), kind=kOutput, calls=%fused_computation.90 | convolution fusion | flops 281018880 | bytes 17858560 | tf_op jit(solution)/shard_map/sub | solution.py:45
  34.6 0.0 copy-start.5
  34.6 0.0 copy-start.6
  34.6 0.0 copy-start.7
  34.6 0.0 copy-start.2
  34.6 0.0 copy-start.4
  34.6 7.5 %fusion.15 = bf16[16,32,512]{2,1,0:T(8,128)(2,1)S(1)} fusion(bf16[512,16,32]{0,2,1:T(8,128)(2,1)S(1)} %bitcast.86, f32[16,512,512]{1,2,0:T(8,128)} %get-tuple-element.15, f32[16,512]{1,0:T(8,128)S(1)} %get-tuple-element.14), kind=kOutput, calls=%fused_computation.36 | convolution fusion | flops 277086208 | bytes 17858560 | tf_op jit(solution)/shard_map/hqk,khd->qhd/dot_general | solution.py:47
  42.0 0.0 copy-done.5
  42.1 0.5 fusion.19
  42.6 0.0 copy-done.6
  42.6 0.0 copy-done.7
  42.6 1.3 %convolution_convert_fusion.2 = bf16[512,512]{0,1:T(8,128)(2,1)} fusion(bf16[512,512]{1,0:T(8,128)(2,1)S(1)} %copy-done.6, bf16[512,512]{0,1:T(8,128)(2,1)S(1)} %get-tuple-element.17, f32[512]{0:T(512)S(1)} %copy-done.7, f32[512]{0:T(512)S(1)} %add_rsqrt_fusion), kind=kOutput, calls=%fused_computation.31 | convolution fusion | flops 269746176 | bytes 1576960 | tf_op jit(solution)/shard_map/dot_general | solution.py:32
  44.0 1.3 %copy.51 = bf16[1,512,512]{1,2,0:T(8,128)(2,1)S(1)} copy(bf16[1,512,512]{2,1,0:T(8,128)(2,1)} %param.17) | data formatting | bytes 1048576 | tf_op args[1]
  45.2 0.5 concatenate.7
  45.8 2.0 %scatter_custom_fusion.1 = bf16[256,128]{1,0:T(8,128)(2,1)} fusion(s32[256]{0:T(256)S(1)} %bitcast.98, bf16[256,128]{1,0:T(8,128)(2,1)} %param.31, bf16[]{:T(256)} %constant.14.clone.1), kind=kCustom, calls=%fused_computation.60 | custom fusion | bytes 66048 | tf_op jit(solution)/shard_map/scatter | solution.py:98
  47.8 0.0 all-to-all-done
  47.8 6.0 %all-to-all-start.1 = ((bf16[16,16,128]{2,1,0:T(8,128)(2,1)}), bf16[16,16,128]{2,1,0:T(8,128)(2,1)}, u32[]{:S(2)}, u32[]{:S(2)}) async-start(bf16[16,16,128]{2,1,0:T(8,128)(2,1)} %bitcast.19), calls=%async_computation.1 | async-start | bytes 131072 | tf_op jit(solution)/shard_map/all_to_all | solution.py:107
  53.9 0.5 broadcast.169
  54.4 0.6 broadcast_minimum_fusion
  55.1 0.1 reshape.167
  55.2 0.1 reshape.162
  55.3 0.0 copy-done.2
  55.3 1.2 %gather_fusion = bf16[256,512]{1,0:T(8,128)(2,1)S(1)} fusion(bf16[512,512]{1,0:T(8,128)(2,1)S(1)} %bitcast.85, s32[1024]{0:T(1024)S(1)} %pad_clamp_fusion), kind=kCustom, calls=%fused_computation | custom fusion | bytes 525312 | tf_op jit(solution)/shard_map/jit(_take)/gather | solution.py:110
  56.4 4.4 %all-to-all-done.1 = bf16[16,16,128]{2,1,0:T(8,128)(2,1)} async-done(((bf16[16,16,128]{2,1,0:T(8,128)(2,1)}), bf16[16,16,128]{2,1,0:T(8,128)(2,1)}, u32[]{:S(2)}, u32[]{:S(2)}) %all-to-all-start.1) | async-done | bytes 65568 | tf_op jit(solution)/shard_map/all_to_all | solution.py:107
  60.8 0.0 copy-done.4
  60.8 1.1 %fusion.18 = f32[16,16,128]{2,1,0:T(8,128)S(1)} fusion(bf16[16,16,512]{2,1,0:T(8,128)(2,1)S(1)} %bitcast.90, pred[16,16]{1,0:T(8,128)(4,1)S(1)} %compare_and_fusion, bf16[512,128]{1,0:T(8,128)(2,1)S(1)} %copy-done.4, bf16[16,16,128]{2,1,0:T(8,128)(2,1)} %all-to-all-done.1, pred[16,16]{1,0:T(8,128)(4,1)S(1)} %compare_bitcast_fusion), kind=kOutput, calls=%fused_computation.40 | convolution fusion | flops 33816576 | bytes 590336 | tf_op jit(solution)/shard_map/ncd,do->nco/dot_general | solution.py:111
  62.0 1.7 %scatter_custom_fusion.2 = f32[512,128]{1,0:T(8,128)S(1)} fusion(s32[256]{0:T(256)S(1)} %bitcast.99, f32[256,128]{1,0:T(8,128)S(1)} %bitcast.100, f32[]{:T(128)} %constant.19.clone.1), kind=kCustom, calls=%fused_computation.58 | custom fusion | flops 32768 | bytes 262148 | tf_op jit(solution)/shard_map/scatter-add | solution.py:118
  63.6 0.0 collective-permute-done
  63.7 1.1 %constant_dynamic-update-slice_fusion.1 = bf16[1024,512]{0,1:T(8,128)(2,1)S(1)} fusion(bf16[512,512]{0,1:T(8,128)(2,1)} %collective-permute-done), kind=kLoop, calls=%fused_computation.78 | loop fusion | bytes 1048576
  64.8 0.0 collective-permute-done.1
  64.8 1.1 %constant_dynamic-update-slice_fusion = bf16[1024,512]{0,1:T(8,128)(2,1)S(1)} fusion(bf16[1024,512]{0,1:T(8,128)(2,1)S(1)} %constant_dynamic-update-slice_fusion.1, bf16[512,512]{0,1:T(8,128)(2,1)} %collective-permute-done.1), kind=kLoop, calls=%fused_computation.77 | loop fusion | bytes 1048576 | tf_op jit(solution)/shard_map/concatenate | solution.py:83
  65.9 0.0 copy-done
  65.9 1.8 %convolution_convert_fusion = bf16[1024,512]{0,1:T(8,128)(2,1)} fusion(bf16[1024,512]{0,1:T(8,128)(2,1)S(1)} %constant_dynamic-update-slice_fusion, bf16[512,512]{1,0:T(8,128)(2,1)S(1)} %copy-done), kind=kOutput, calls=%fused_computation.28 | convolution fusion | flops 537395200 | bytes 2621440 | tf_op jit(solution)/shard_map/dot_general | solution.py:32
  67.7 2.8 %convolution_convert_fusion.1 = bf16[1024,512]{0,1:T(8,128)(2,1)} fusion(bf16[1024,512]{0,1:T(8,128)(2,1)S(1)} %constant_dynamic-update-slice_fusion, bf16[512,512]{1,0:T(8,128)(2,1)} %param.26), kind=kOutput, calls=%fused_computation.29 | convolution fusion | flops 537395200 | bytes 2621440 | tf_op jit(solution)/shard_map/dot_general | solution.py:32
  70.4 16.4 %fusion.52 = (f32[16,512]{1,0:T(8,128)}, f32[16,512,1024]{2,1,0:T(8,128)}) fusion(pred[1024]{0:T(1024)(128)(4,1)} %concatenate.7, bf16[512,16,32]{0,2,1:T(8,128)(2,1)} %bitcast.103, bf16[1024,16,32]{0,2,1:T(8,128)(2,1)} %bitcast.102), kind=kOutput, calls=%fused_computation.91 | convolution fusion | flops 570426368 | bytes 35161088 | tf_op jit(solution)/shard_map/sub | solution.py:45
  86.8 0.0 copy-start.3
  86.8 0.0 copy-start.1
  86.8 13.7 %fusion.16 = bf16[16,32,512]{2,1,0:T(8,128)(2,1)S(1)} fusion(bf16[1024,16,32]{0,2,1:T(8,128)(2,1)} %bitcast.101, f32[16,512,1024]{2,1,0:T(8,128)} %get-tuple-element.19, f32[16,512]{1,0:T(8,128)} %get-tuple-element.18), kind=kOutput, calls=%fused_computation.37 | convolution fusion | flops 553910272 | bytes 35160064 | tf_op jit(solution)/shard_map/hqk,khd->qhd/dot_general | solution.py:47
  100.5 0.0 copy-done.3
  100.5 0.5 convert_add_fusion.2
  101.0 0.4 fusion.27
  101.4 1.0 copy.52
  102.4 1.0 copy.53
  103.4 0.0 copy-done.1
  (11 shorter events, 0.1 us)
Async XLA Ops:
  0.6 65.3 %copy-start = (bf16[512,512]{1,0:T(8,128)(2,1)S(1)}, bf16[512,512]{1,0:T(8,128)(2,1)}, u32[]{:S(2)}) copy-start(bf16[512,512]{1,0:T(8,128)(2,1)} %param.25) | copy-start | bytes 1572868
  3.0 60.7 %collective-permute-start = (bf16[512,512]{0,1:T(8,128)(2,1)S(1)}, bf16[512,512]{0,1:T(8,128)(2,1)}, u32[]{:S(2)}, u32[]{:S(2)}) collective-permute-start(bf16[512,512]{0,1:T(8,128)(2,1)S(1)} %fusion.24), channel_id=1, source_target_pairs={{0,1},{1,2},{2,3},{3,4},{4,5},{5,6},{6,7},{7,8},{8,9},{9,10},{10,1... | collective-permute-start | bytes 1572872 | tf_op jit(solution)/shard_map/ppermute | solution.py:21
  6.2 58.6 %collective-permute-start.1 = (bf16[512,512]{0,1:T(8,128)(2,1)S(1)}, bf16[512,512]{0,1:T(8,128)(2,1)}, u32[]{:S(2)}, u32[]{:S(2)}) collective-permute-start(bf16[512,512]{0,1:T(8,128)(2,1)S(1)} %fusion.24), channel_id=1, source_target_pairs={{1,0},{2,1},{3,2},{4,3},{5,4},{6,5},{7,6},{8,7},{9,8},{10,9},{11,1... | collective-permute-start | bytes 1572872 | tf_op jit(solution)/shard_map/ppermute | solution.py:21
  12.6 35.2 %all-to-all-start = ((s32[16,1,16]{2,1,0:T(1,128)}), s32[16,1,16]{2,1,0:T(1,128)S(1)}, u32[]{:S(2)}, u32[]{:S(2)}) async-start(s32[16,1,16]{2,1,0:T(1,128)} %all_to_all.9), calls=%async_computation | async-start | bytes 16384 | tf_op jit(solution)/shard_map/all_to_all | solution.py:108
  34.6 7.5 %copy-start.5 = (bf16[512,512]{1,0:T(8,128)(2,1)S(1)}, bf16[512,512]{1,0:T(8,128)(2,1)}, u32[]{:S(2)}) copy-start(bf16[512,512]{1,0:T(8,128)(2,1)} %param.23) | copy-start | bytes 1572868
  34.6 8.0 %copy-start.6 = (bf16[512,512]{1,0:T(8,128)(2,1)S(1)}, bf16[512,512]{1,0:T(8,128)(2,1)}, u32[]{:S(2)}) copy-start(bf16[512,512]{1,0:T(8,128)(2,1)} %param.24) | copy-start | bytes 1572868
  34.6 8.1 %copy-start.7 = (f32[512]{0:T(512)S(1)}, f32[512]{0:T(512)}, u32[]{:S(2)}) copy-start(f32[512]{0:T(512)} %param.19) | copy-start | bytes 6148
  34.6 20.7 %copy-start.2 = (bf16[1,512,512]{2,1,0:T(8,128)(2,1)S(1)}, bf16[1,512,512]{2,1,0:T(8,128)(2,1)}, u32[]{:S(2)}) copy-start(bf16[1,512,512]{2,1,0:T(8,128)(2,1)} %param.16) | copy-start | bytes 1572868
  34.6 26.3 %copy-start.4 = (bf16[512,128]{1,0:T(8,128)(2,1)S(1)}, bf16[512,128]{1,0:T(8,128)(2,1)}, u32[]{:S(2)}) copy-start(bf16[512,128]{1,0:T(8,128)(2,1)} %param.28) | copy-start | bytes 393220
  47.8 13.0 %all-to-all-start.1 = ((bf16[16,16,128]{2,1,0:T(8,128)(2,1)}), bf16[16,16,128]{2,1,0:T(8,128)(2,1)}, u32[]{:S(2)}, u32[]{:S(2)}) async-start(bf16[16,16,128]{2,1,0:T(8,128)(2,1)} %bitcast.19), calls=%async_computation.1 | async-start | bytes 131072 | tf_op jit(solution)/shard_map/all_to_all | solution.py:107
  86.8 13.7 %copy-start.3 = (bf16[512,512]{1,0:T(8,128)(2,1)S(1)}, bf16[512,512]{1,0:T(8,128)(2,1)}, u32[]{:S(2)}) copy-start(bf16[512,512]{1,0:T(8,128)(2,1)} %param.27) | copy-start | bytes 1572868
  86.8 16.6 %copy-start.1 = (bf16[512,512]{1,0:T(8,128)(2,1)S(1)}, bf16[512,512]{1,0:T(8,128)(2,1)}, u32[]{:S(2)}) copy-start(bf16[512,512]{1,0:T(8,128)(2,1)} %param.25) | copy-start | bytes 1572868
where the time goes:
time: 104 us; the launch traced here: 103 us
  matrix products  59.3 us (57%)
  starting transfers between devices  19 us (18%)
  local copies, waits for them, and re-layouts  13.7 us (13%)
  other arithmetic  6.08 us (6%)
  waiting for transfers between devices  4.4 us (4%)
    sub x2, matrix products, attend(): exponent = jnp.exp(scores - largest)  25.2 us
    dot_general x2, matrix products, attend(): jnp.einsum('hqk,khd->qhd', weights, vb, preferred_element_type=jnp.float32)  21.1 us
    dot_general x8, matrix products, linear(): return jnp.dot(array, matrix, preferred_element_type=jnp.float32)  11.5 us
    all_to_all x1, starting transfers between devices, per_device(): lax.all_to_all(send_row, 'tm', split_axis=0, concat_axis=0, tiled=True)  8.51 us
    all_to_all x1, starting transfers between devices, per_device(): lax.all_to_all(send_value, 'tm', split_axis=0, concat_axis=0, tiled=True)  6.05 us
    unnamed x21, local copies, waits for them, and re-layouts  5.74 us
    ppermute x2, starting transfers between devices, shifted(): return lax.ppermute(array, axis, pairs)  4.48 us
    all_to_all x1, waiting for transfers between devices, per_device(): lax.all_to_all(send_value, 'tm', split_axis=0, concat_axis=0, tiled=True)  4.39 us
  transfers between devices with their start and end apart: 4, of which 1 were waited for; matrix products, arithmetic and copies ran while one was open for 36% of the time, Pallas kernels for 0%

commit v1 on v0

v1 whole, which is shorter than its diff:
```python
import functools
import math

import jax
import jax.numpy as jnp
from jax import lax
from jax.experimental import pallas as pl
from jax.experimental.pallas import tpu as pltpu
from jax.sharding import PartitionSpec as P

HEADS = 16
CAP = 16
LANES = 128

step_size = 0.1
inv_var = 2.0
MESH = pl.DeviceIdType.MESH
NT = (((1,), (1,)), ((), ()))
TN = (((0,), (0,)), ((), ()))


def matmul(a, b):
    return jnp.dot(a, b, preferred_element_type=jnp.float32)


def rms_norm(rows, gain):
    rows = rows.astype(jnp.float32)
    scale = lax.rsqrt(jnp.mean(rows * rows, axis=-1, keepdims=True) + 1e-05)
    return (rows * scale * gain).astype(jnp.bfloat16)


def attend_block(q_ref, kv_refs, out_ref, lanes, head_size):
    q_block = q_ref[:, lanes]
    lane = lax.broadcasted_iota(jnp.int32, (1, LANES), 1) // head_size
    factor = head_size ** (-0.5) * math.log2(math.e)
    total = None
    for h in range(LANES // head_size):
        own = lane == h
        q_head = jnp.where(own, q_block, jnp.zeros_like(q_block))
        scores = [
            lax.dot_general(q_head, k[:, lanes], NT, preferred_element_type=jnp.float32)
            for k, _ in kv_refs
        ]
        largest = functools.reduce(
            jnp.maximum, [jnp.max(s, axis=-1, keepdims=True) for s in scores]
        )
        for s, (_, v) in zip(scores, kv_refs):
            weights = jnp.exp2(((s - largest) * factor).astype(jnp.bfloat16))
            v_block = v[:, lanes]
            v_head = jnp.where(own, v_block, jnp.zeros_like(v_block))
            ones = jnp.broadcast_to(own, v_block.shape).astype(jnp.bfloat16)
            part = matmul(weights, jnp.concatenate([v_head, ones], axis=1))
            total = part if total is None else total + part
    out_ref[:, lanes] = (total[:, :LANES] / total[:, LANES:]).astype(jnp.bfloat16)


def attend(q_ref, kv_refs, out_ref):
    width = q_ref.shape[1]
    head_size = width // HEADS

    @pl.loop(0, width // LANES)
    def _(block):
        lanes = pl.ds(pl.multiple_of(block * LANES, LANES), LANES)
        attend_block(q_ref, kv_refs, out_ref, lanes, head_size)


def kernel(
    n,
    state_hbm, noise_hbm, gain_first, gain_second,
    wq_hbm, wk_hbm, wv_hbm, wo_hbm, cq_hbm, ck_hbm, cv_hbm, co_hbm,
    operator, owner_ref, row_ref, value_ref,
    drift_ref, updated_ref,
    x, noise, wq, wk, wv, wo, cq, ck, cv, co,
    before, after, normed, q, k, v, att, mid, kb, vb, ka, va, message, inbox,
    load_sem, near_send, near_recv, obs_send, obs_recv,
):
    me = lax.axis_index("tm")
    token_count = x.shape[0]
    obs_count = value_ref.shape[0]

    sources = [state_hbm, wq_hbm, wk_hbm, wv_hbm, wo_hbm, cq_hbm, ck_hbm, cv_hbm, co_hbm, noise_hbm]
    targets = [x, wq, wk, wv, wo, cq, ck, cv, co, noise]
    loads = [pltpu.make_async_copy(s, t, load_sem.at[i]) for i, (s, t) in enumerate(zip(sources, targets))]
    for load in loads:
        load.start()
    load_x, load_wq, load_wk, load_wv, load_wo, load_cq, load_ck, load_cv, load_co, load_noise = loads

    barrier = pltpu.get_barrier_semaphore()

    @pl.loop(1, n)
    def _(offset):
        peer = lax.rem(me + offset, n)
        pl.semaphore_signal(barrier, inc=1, device_id={"tm": peer}, device_id_type=MESH)

    owner = owner_ref[...]
    onehot = lax.broadcasted_iota(jnp.int32, (n, obs_count), 0) == owner
    earlier = lax.broadcasted_iota(jnp.int32, (obs_count, obs_count), 0) <= lax.broadcasted_iota(
        jnp.int32, (obs_count, obs_count), 1
    )
    running = matmul(onehot.astype(jnp.bfloat16), earlier.astype(jnp.bfloat16))
    place = jnp.sum(jnp.where(onehot, running, 0.0), axis=0, keepdims=True) - 1.0
    destination = owner * CAP + place.astype(jnp.int32)
    routed = lax.broadcasted_iota(jnp.int32, (n * CAP, obs_count), 0) == destination
    values = matmul(routed.astype(jnp.bfloat16), value_ref[...])
    row = row_ref[...]
    high = jnp.sum(jnp.where(routed, ((row >> 8) + 1).astype(jnp.float32), 0.0), axis=1, keepdims=True) - 1.0
    low = jnp.sum(jnp.where(routed, (row & 255).astype(jnp.float32), 0.0), axis=1, keepdims=True)
    side = lax.broadcasted_iota(jnp.int32, (n * CAP, LANES), 1)
    codes = jnp.where(side == 0, high, low)
    message[...] = (
        jnp.concatenate([values, codes], axis=1).astype(jnp.bfloat16).reshape(message.shape)
    )

    load_x.wait()
    normed[...] = rms_norm(x[...], gain_first[...])

    pl.semaphore_wait(barrier, n - 1)
    to_next = pltpu.make_async_remote_copy(
        src_ref=state_hbm, dst_ref=before, send_sem=near_send.at[0], recv_sem=near_recv.at[0],
        device_id={"tm": lax.rem(me + 1, n)}, device_id_type=MESH,
    )
    to_last = pltpu.make_async_remote_copy(
        src_ref=state_hbm, dst_ref=after, send_sem=near_send.at[1], recv_sem=near_recv.at[1],
        device_id={"tm": lax.rem(me + n - 1, n)}, device_id_type=MESH,
    )

    @pl.when(me < n - 1)
    def _():
        to_next.start()

    @pl.when(me > 0)
    def _():
        to_last.start()

    load_wq.wait()
    q[...] = matmul(normed[...], wq[...]).astype(jnp.bfloat16)
    load_wk.wait()
    k[...] = matmul(normed[...], wk[...]).astype(jnp.bfloat16)
    load_wv.wait()
    v[...] = matmul(normed[...], wv[...]).astype(jnp.bfloat16)

    def observation_copy(offset):
        peer = lax.rem(me + offset, n)
        return pltpu.make_async_remote_copy(
            src_ref=message.at[peer], dst_ref=inbox.at[me],
            send_sem=obs_send.at[offset], recv_sem=obs_recv.at[offset],
            device_id={"tm": peer}, device_id_type=MESH,
        )

    @pl.loop(1, n)
    def _(offset):
        observation_copy(offset).start()

    attend(q, [(k, v)], att)
    load_wo.wait()
    middle = (x[...].astype(jnp.float32) + matmul(att[...], wo[...])).astype(jnp.bfloat16)
    mid[...] = middle
    lifted = rms_norm(middle, gain_second[...])
    load_cq.wait()
    q[...] = matmul(lifted, cq[...]).astype(jnp.bfloat16)

    @pl.when(me > 0)
    def _():
        to_next.wait_recv()

    @pl.when(me < n - 1)
    def _():
        to_last.wait_recv()

    @pl.when(me == 0)
    def _():
        before[...] = after[...]

    @pl.when(me == n - 1)
    def _():
        after[...] = before[...]

    load_ck.wait()
    load_cv.wait()
    for rows, keys, vals in ((before, kb, vb), (after, ka, va)):
        near = rms_norm(rows[...], gain_first[...])
        keys[...] = matmul(near, ck[...]).astype(jnp.bfloat16)
        vals[...] = matmul(near, cv[...]).astype(jnp.bfloat16)
    attend(q, [(kb, vb), (ka, va)], att)

    @pl.when(me < n - 1)
    def _():
        to_next.wait_send()

    @pl.when(me > 0)
    def _():
        to_last.wait_send()

    @pl.loop(1, n)
    def _(offset):
        observation_copy(offset).wait()

    inbox[me] = message[me]

    arrived = inbox[...].reshape(n * CAP, 2 * LANES)
    codes_in = arrived[:, LANES:].astype(jnp.float32)
    rows_in = (codes_in[:, 0:1] * 256.0 + codes_in[:, 1:2]).astype(jnp.int32)
    hit = (rows_in == lax.broadcasted_iota(jnp.int32, (n * CAP, token_count), 1)).astype(jnp.bfloat16)
    gathered = lax.dot_general(
        hit,
        jnp.concatenate([arrived[:, :LANES], jnp.ones((n * CAP, LANES), jnp.bfloat16)], axis=1),
        TN, preferred_element_type=jnp.float32,
    )
    predicted = matmul(x[...], operator[...])
    token_misfit = (
        inv_var * (gathered[:, :LANES] - gathered[:, LANES:] * predicted)
    ).astype(jnp.bfloat16)
    gradient = lax.dot_general(token_misfit, operator[...], NT, preferred_element_type=jnp.float32)
    load_co.wait()
    combined = mid[...].astype(jnp.float32) + matmul(att[...], co[...]) + gradient
    drift_ref[...] = combined.astype(jnp.bfloat16)
    load_noise.wait()
    updated_ref[...] = (
        x[...].astype(jnp.float32)
        + step_size * combined
        + math.sqrt(2.0 * step_size) * noise[...].astype(jnp.float32)
    ).astype(jnp.bfloat16)


def per_device(
    state, noise, gain_first, gain_second,
    self_query, self_key, self_value, self_out,
    cross_query, cross_key, cross_value, cross_out,
    obs_operator, obs_owner, obs_row, obs_value,
):
    n = lax.axis_size("tm")
    tokens = state[0]
    token_count, width = tokens.shape
    obs_count, channels = obs_value.shape
    hbm = pl.BlockSpec(memory_space=pl.ANY)
    vmem = pl.BlockSpec(memory_space=pltpu.VMEM)
    rows = pltpu.VMEM((token_count, width), jnp.bfloat16)
    square = pltpu.VMEM((width, width), jnp.bfloat16)
    box = pltpu.VMEM((n, CAP, channels + LANES), jnp.bfloat16)
    out = jax.ShapeDtypeStruct((token_count, width), jnp.bfloat16)
    drift, updated = pl.pallas_call(
        functools.partial(kernel, n),
        name="langevin",
        out_shape=(out, out),
        in_specs=[hbm, hbm, vmem, vmem] + [hbm] * 8 + [vmem] * 4,
        out_specs=(vmem, vmem),
        scratch_shapes=[rows, rows] + [square] * 8 + [rows] * 12 + [
            box, box,
            pltpu.SemaphoreType.DMA((10,)),
            pltpu.SemaphoreType.DMA((2,)),
            pltpu.SemaphoreType.DMA((2,)),
            pltpu.SemaphoreType.DMA((n,)),
            pltpu.SemaphoreType.DMA((n,)),
        ],
        compiler_params=pltpu.CompilerParams(
            collective_id=0, has_side_effects=True, vmem_limit_bytes=56 * 1024 * 1024
        ),
    )(
        tokens, noise[0], gain_first[None, :], gain_second[None, :],
        self_query, self_key, self_value, self_out,
        cross_query, cross_key, cross_value, cross_out,
        obs_operator, obs_owner.reshape(1, obs_count), obs_row.reshape(1, obs_count), obs_value,
    )
    return (drift[None], updated[None])


def solution(mesh):
    split = P(("group", "tm"), None, None)
    return jax.shard_map(
        per_device,
        mesh=mesh,
        in_specs=(split, split) + (P(),) * 11 + (
            P(("group", "tm"), None),
            P(("group", "tm")),
            P(("group", "tm"), None),
        ),
        out_specs=(split, split),
        check_vma=False,
    )
```

time: 104 us -> 40.4 us (0.39)
  the two profiles are of different devices: /device:TPU:0 before, /device:TPU:4 now
where the time goes in v1:
time: 40.4 us; the launch traced here: 40.2 us
  Pallas kernels  36.8 us (91%)
  local copies, waits for them, and re-layouts  2.72 us (7%)
  between operations  0.65 us (2%)
    pallas_call x1, Pallas kernels, per_device(): pl.pallas_call(functools.partial(kernel, n), name='langevin', out_shape=(...  36.8 us
    unnamed x4, local copies, waits for them, and re-layouts  2.72 us

profile of v1, /device:TPU:4, one launch (start us, length us, event | category | flops | bytes accessed | tf_op | source)
XLA Modules:
  0.0 40.2 jit_solution(14846240891440049316)
XLA Ops:
  0.6 36.8 %langevin.1 = (bf16[512,512]{1,0:T(8,128)(2,1)}, bf16[512,512]{1,0:T(8,128)(2,1)}) custom-call(bf16[512,512]{1,0:T(8,128)(2,1)} %bitcast.8, bf16[512,512]{1,0:T(8,128)(2,1)} %bitcast.9, f32[1,512]{1,0:T(1,128)} %bitcast.12, f32[1,512]{1,0:T(1,128)} %bitcast.13, bf16[512,512]{1,0:T(8,128)(2,1)} %wq_hbm.1, bf16[512,512]{1,0:T(8,128)(2,1)} %wk_hbm.1, ...), custom_call_target="tpu_custom_call" | custom-call | tf_op jit(solution)/shard_map/langevin/pallas_call | solution.py:241
  37.5 0.0 copy-start
  37.5 1.9 %copy.20 = bf16[1,512,512]{2,1,0:T(8,128)(2,1)} copy(bf16[1,512,512]{2,1,0:T(8,128)(2,1)} %bitcast.11) | data formatting | bytes 1048576
  39.4 0.0 copy-done
  39.4 0.8 %copy.21 = bf16[1,512,512]{2,1,0:T(8,128)(2,1)} copy(bf16[1,512,512]{2,1,0:T(8,128)(2,1)S(1)} %bitcast.10) | data formatting | bytes 1048576
Async XLA Ops:
  37.5 1.9 %copy-start = (bf16[512,512]{1,0:T(8,128)(2,1)S(1)}, bf16[512,512]{1,0:T(8,128)(2,1)}, u32[]{:S(2)}) copy-start(bf16[512,512]{1,0:T(8,128)(2,1)} %get-tuple-element.5) | copy-start | bytes 1572868

commit v2 on v1

--- a/solution.py
+++ b/solution.py
@@ -10,6 +10,7 @@
 
 HEADS = 16
 CAP = 16
+CHUNK = 256
 LANES = 128
 
 step_size = 0.1
@@ -29,39 +30,61 @@
     return (rows * scale * gain).astype(jnp.bfloat16)
 
 
-def attend_block(q_ref, kv_refs, out_ref, lanes, head_size):
-    q_block = q_ref[:, lanes]
+def attend(q_ref, kv_refs, out_ref, score_refs, peak_refs):
+    token_count, width = q_ref.shape
+    head_size = width // HEADS
+    per_block = LANES // head_size
+    blocks = width // LANES
+    factor = head_size ** (-0.5) * math.log2(math.e)
     lane = lax.broadcasted_iota(jnp.int32, (1, LANES), 1) // head_size
-    factor = head_size ** (-0.5) * math.log2(math.e)
-    total = None
-    for h in range(LANES // head_size):
-        own = lane == h
-        q_head = jnp.where(own, q_block, jnp.zeros_like(q_block))
-        scores = [
-            lax.dot_general(q_head, k[:, lanes], NT, preferred_element_type=jnp.float32)
-            for k, _ in kv_refs
-        ]
-        largest = functools.reduce(
-            jnp.maximum, [jnp.max(s, axis=-1, keepdims=True) for s in scores]
+    ones = jnp.ones((16, CHUNK), jnp.bfloat16)
+    chunks = [(k, v, c * CHUNK) for k, v in kv_refs for c in range(token_count // CHUNK)]
+
+    def head_queries(block, h):
+        lanes = pl.ds(pl.multiple_of(block * LANES, LANES), LANES)
+        q_block = q_ref[:, lanes]
+        return jnp.where(lane == h, q_block, jnp.zeros_like(q_block)), lanes
+
+    def score(index, q_head, lanes, slot, peak):
+        k, _, start = chunks[index]
+        part = lax.dot_general(
+            k[start : start + CHUNK, lanes], q_head, NT, preferred_element_type=jnp.float32
         )
-        for s, (_, v) in zip(scores, kv_refs):
-            weights = jnp.exp2(((s - largest) * factor).astype(jnp.bfloat16))
-            v_block = v[:, lanes]
-            v_head = jnp.where(own, v_block, jnp.zeros_like(v_block))
-            ones = jnp.broadcast_to(own, v_block.shape).astype(jnp.bfloat16)
-            part = matmul(weights, jnp.concatenate([v_head, ones], axis=1))
+        score_refs[slot][index * CHUNK : (index + 1) * CHUNK, :] = part
+        top = jnp.max(part.reshape(CHUNK // 8, 8, token_count), axis=0)
+        return top if peak is None else jnp.maximum(peak, top)
+
+    def stage(block, h, next_block, next_h):
+        slot, next_slot = h % 2, next_h % 2
+        q_head, lanes = head_queries(next_block, next_h)
+        largest = jnp.max(peak_refs[slot][...], axis=0, keepdims=True)
+        features = pl.ds(pl.multiple_of(block * LANES + h * head_size, head_size), head_size)
+        total, peak = None, None
+        for index, (_, v, start) in enumerate(chunks):
+            peak = score(index, q_head, lanes, next_slot, peak)
+            part = score_refs[slot][index * CHUNK : (index + 1) * CHUNK, :]
+            weights = jnp.exp2(((part - largest) * factor).astype(jnp.bfloat16))
+            rows = jnp.concatenate([v[features, start : start + CHUNK], ones], axis=0)
+            part = matmul(rows, weights)
             total = part if total is None else total + part
-    out_ref[:, lanes] = (total[:, :LANES] / total[:, LANES:]).astype(jnp.bfloat16)
-
-
-def attend(q_ref, kv_refs, out_ref):
-    width = q_ref.shape[1]
-    head_size = width // HEADS
-
-    @pl.loop(0, width // LANES)
+        peak_refs[next_slot][...] = peak
+        out_ref[features, :] = (
+            total[:head_size] / total[head_size : head_size + 1]
+        ).astype(jnp.bfloat16)
+
+    q_head, lanes = head_queries(0, 0)
+    peak = None
+    for index in range(len(chunks)):
+        peak = score(index, q_head, lanes, 0, peak)
+    peak_refs[0][...] = peak
+
+    @pl.loop(0, blocks)
     def _(block):
-        lanes = pl.ds(pl.multiple_of(block * LANES, LANES), LANES)
-        attend_block(q_ref, kv_refs, out_ref, lanes, head_size)
+        for h in range(per_block):
+            if h < per_block - 1:
+                stage(block, h, block, h + 1)
+            else:
+                stage(block, h, jnp.minimum(block + 1, blocks - 1), 0)
 
 
 def kernel(
@@ -72,6 +95,7 @@
     drift_ref, updated_ref,
     x, noise, wq, wk, wv, wo, cq, ck, cv, co,
     before, after, normed, q, k, v, att, mid, kb, vb, ka, va, message, inbox,
+    scores_a, scores_b, peak_a, peak_b,
     load_sem, near_send, near_recv, obs_send, obs_recv,
 ):
     me = lax.axis_index("tm")
@@ -137,7 +161,7 @@
     load_wk.wait()
     k[...] = matmul(normed[...], wk[...]).astype(jnp.bfloat16)
     load_wv.wait()
-    v[...] = matmul(normed[...], wv[...]).astype(jnp.bfloat16)
+    v[...] = matmul(normed[...], wv[...]).astype(jnp.bfloat16).T
 
     def observation_copy(offset):
         peer = lax.rem(me + offset, n)
@@ -151,9 +175,9 @@
     def _(offset):
         observation_copy(offset).start()
 
-    attend(q, [(k, v)], att)
+    attend(q, [(k, v)], att, (scores_a, scores_b), (peak_a, peak_b))
     load_wo.wait()
-    middle = (x[...].astype(jnp.float32) + matmul(att[...], wo[...])).astype(jnp.bfloat16)
+    middle = (x[...].astype(jnp.float32) + lax.dot_general(att[...], wo[...], TN, preferred_element_type=jnp.float32)).astype(jnp.bfloat16)
     mid[...] = middle
     lifted = rms_norm(middle, gain_second[...])
     load_cq.wait()
@@ -180,8 +204,8 @@
     for rows, keys, vals in ((before, kb, vb), (after, ka, va)):
         near = rms_norm(rows[...], gain_first[...])
         keys[...] = matmul(near, ck[...]).astype(jnp.bfloat16)
-        vals[...] = matmul(near, cv[...]).astype(jnp.bfloat16)
-    attend(q, [(kb, vb), (ka, va)], att)
+        vals[...] = matmul(near, cv[...]).astype(jnp.bfloat16).T
+    attend(q, [(kb, vb), (ka, va)], att, (scores_a, scores_b), (peak_a, peak_b))
 
     @pl.when(me < n - 1)
     def _():
@@ -212,7 +236,7 @@
     ).astype(jnp.bfloat16)
     gradient = lax.dot_general(token_misfit, operator[...], NT, preferred_element_type=jnp.float32)
     load_co.wait()
-    combined = mid[...].astype(jnp.float32) + matmul(att[...], co[...]) + gradient
+    combined = mid[...].astype(jnp.float32) + lax.dot_general(att[...], co[...], TN, preferred_element_type=jnp.float32) + gradient
     drift_ref[...] = combined.astype(jnp.bfloat16)
     load_noise.wait()
     updated_ref[...] = (
@@ -237,6 +261,8 @@
     rows = pltpu.VMEM((token_count, width), jnp.bfloat16)
     square = pltpu.VMEM((width, width), jnp.bfloat16)
     box = pltpu.VMEM((n, CAP, channels + LANES), jnp.bfloat16)
+    scores = pltpu.VMEM((2 * token_count, token_count), jnp.float32)
+    peak = pltpu.VMEM((8, token_count), jnp.float32)
     out = jax.ShapeDtypeStruct((token_count, width), jnp.bfloat16)
     drift, updated = pl.pallas_call(
         functools.partial(kernel, n),
@@ -246,6 +272,7 @@
         out_specs=(vmem, vmem),
         scratch_shapes=[rows, rows] + [square] * 8 + [rows] * 12 + [
             box, box,
+            scores, scores, peak, peak,
             pltpu.SemaphoreType.DMA((10,)),
             pltpu.SemaphoreType.DMA((2,)),
             pltpu.SemaphoreType.DMA((2,)),

time: 40.4 us -> 39.8 us (0.985)
  Pallas kernels: 36.8 us -> 36.3 us
    pallas_call x1, Pallas kernels: 36.8 us -> 36.3 us  [per_device(): pl.pallas_call(functools.partial(kernel, n), name='langevin', out_shape=(...]
where the time goes in v2:
time: 39.8 us; the launch traced here: 39.7 us
  Pallas kernels  36.3 us (91%)
  local copies, waits for them, and re-layouts  2.72 us (7%)
  between operations  0.65 us (2%)
    pallas_call x1, Pallas kernels, per_device(): pl.pallas_call(functools.partial(kernel, n), name='langevin', out_shape=(...  36.3 us
    unnamed x4, local copies, waits for them, and re-layouts  2.72 us

profile of v2, /device:TPU:4, one launch (start us, length us, event | category | flops | bytes accessed | tf_op | source)
XLA Modules:
  0.0 39.7 jit_solution(3173092591386809218)
XLA Ops:
  0.6 36.3 %langevin.1 = (bf16[512,512]{1,0:T(8,128)(2,1)}, bf16[512,512]{1,0:T(8,128)(2,1)}) custom-call(bf16[512,512]{1,0:T(8,128)(2,1)} %bitcast.8, bf16[512,512]{1,0:T(8,128)(2,1)} %bitcast.9, f32[1,512]{1,0:T(1,128)} %bitcast.12, f32[1,512]{1,0:T(1,128)} %bitcast.13, bf16[512,512]{1,0:T(8,128)(2,1)} %wq_hbm.1, bf16[512,512]{1,0:T(8,128)(2,1)} %wk_hbm.1, ...), custom_call_target="tpu_custom_call" | custom-call | tf_op jit(solution)/shard_map/langevin/pallas_call | solution.py:267
  36.9 0.0 copy-start
  36.9 1.9 %copy.20 = bf16[1,512,512]{2,1,0:T(8,128)(2,1)} copy(bf16[1,512,512]{2,1,0:T(8,128)(2,1)} %bitcast.11) | data formatting | bytes 1048576
  38.9 0.0 copy-done
  38.9 0.8 %copy.21 = bf16[1,512,512]{2,1,0:T(8,128)(2,1)} copy(bf16[1,512,512]{2,1,0:T(8,128)(2,1)S(1)} %bitcast.10) | data formatting | bytes 1048576
Async XLA Ops:
  36.9 1.9 %copy-start = (bf16[512,512]{1,0:T(8,128)(2,1)S(1)}, bf16[512,512]{1,0:T(8,128)(2,1)}, u32[]{:S(2)}) copy-start(bf16[512,512]{1,0:T(8,128)(2,1)} %get-tuple-element.5) | copy-start | bytes 1572868

commit v3 on v2

--- a/solution.py
+++ b/solution.py
@@ -30,7 +30,7 @@
     return (rows * scale * gain).astype(jnp.bfloat16)
 
 
-def attend(q_ref, kv_refs, out_ref, score_refs, peak_refs):
+def attend(q_ref, kv_refs, out_ref, score_refs, peak_refs, parts=None, last=True):
     token_count, width = q_ref.shape
     head_size = width // HEADS
     per_block = LANES // head_size
@@ -68,6 +68,18 @@
             part = matmul(rows, weights)
             total = part if total is None else total + part
         peak_refs[next_slot][...] = peak
+        if parts is not None:
+            sums_ref, tops_ref = parts
+            head = block * per_block + h
+            if not last:
+                sums_ref[head] = total
+                tops_ref[head] = jnp.broadcast_to(largest, (8, token_count))
+                return
+            first = tops_ref[head][0:1]
+            joint = jnp.maximum(first, largest)
+            total = sums_ref[head] * jnp.exp2((first - joint) * factor) + total * jnp.exp2(
+                (largest - joint) * factor
+            )
         out_ref[features, :] = (
             total[:head_size] / total[head_size : head_size + 1]
         ).astype(jnp.bfloat16)
@@ -94,8 +106,8 @@
     operator, owner_ref, row_ref, value_ref,
     drift_ref, updated_ref,
     x, noise, wq, wk, wv, wo, cq, ck, cv, co,
-    before, after, normed, q, k, v, att, mid, kb, vb, ka, va, message, inbox,
-    scores_a, scores_b, peak_a, peak_b,
+    near_rows, far_rows, normed, q, k, v, att, mid, kb, vb, message, inbox,
+    scores_a, scores_b, peak_a, peak_b, sums, tops,
     load_sem, near_send, near_recv, obs_send, obs_recv,
 ):
     me = lax.axis_index("tm")
@@ -139,22 +151,23 @@
     normed[...] = rms_norm(x[...], gain_first[...])
 
     pl.semaphore_wait(barrier, n - 1)
-    to_next = pltpu.make_async_remote_copy(
-        src_ref=state_hbm, dst_ref=before, send_sem=near_send.at[0], recv_sem=near_recv.at[0],
-        device_id={"tm": lax.rem(me + 1, n)}, device_id_type=MESH,
-    )
-    to_last = pltpu.make_async_remote_copy(
-        src_ref=state_hbm, dst_ref=after, send_sem=near_send.at[1], recv_sem=near_recv.at[1],
-        device_id={"tm": lax.rem(me + n - 1, n)}, device_id_type=MESH,
-    )
-
-    @pl.when(me < n - 1)
+    odd = lax.rem(me, 2)
+    other = me - 1 + 2 * odd
+    has_other = jnp.logical_and(other >= 0, other < n)
+    to_partner = pltpu.make_async_remote_copy(
+        src_ref=state_hbm, dst_ref=near_rows, send_sem=near_send.at[0], recv_sem=near_recv.at[0],
+        device_id={"tm": me + 1 - 2 * odd}, device_id_type=MESH,
+    )
+    to_other = pltpu.make_async_remote_copy(
+        src_ref=state_hbm, dst_ref=far_rows, send_sem=near_send.at[1], recv_sem=near_recv.at[1],
+        device_id={"tm": lax.rem(other + n, n)}, device_id_type=MESH,
+    )
+
+    @pl.when(has_other)
     def _():
-        to_next.start()
-
-    @pl.when(me > 0)
-    def _():
-        to_last.start()
+        to_other.start()
+
+    to_partner.start()
 
     load_wq.wait()
     q[...] = matmul(normed[...], wq[...]).astype(jnp.bfloat16)
@@ -183,37 +196,27 @@
     load_cq.wait()
     q[...] = matmul(lifted, cq[...]).astype(jnp.bfloat16)
 
-    @pl.when(me > 0)
-    def _():
-        to_next.wait_recv()
-
-    @pl.when(me < n - 1)
-    def _():
-        to_last.wait_recv()
-
-    @pl.when(me == 0)
-    def _():
-        before[...] = after[...]
-
-    @pl.when(me == n - 1)
-    def _():
-        after[...] = before[...]
+    def project_near(rows):
+        normal = rms_norm(rows[...], gain_first[...])
+        kb[...] = matmul(normal, ck[...]).astype(jnp.bfloat16)
+        vb[...] = matmul(normal, cv[...]).astype(jnp.bfloat16).T
 
     load_ck.wait()
     load_cv.wait()
-    for rows, keys, vals in ((before, kb, vb), (after, ka, va)):
-        near = rms_norm(rows[...], gain_first[...])
-        keys[...] = matmul(near, ck[...]).astype(jnp.bfloat16)
-        vals[...] = matmul(near, cv[...]).astype(jnp.bfloat16).T
-    attend(q, [(kb, vb), (ka, va)], att, (scores_a, scores_b), (peak_a, peak_b))
-
-    @pl.when(me < n - 1)
+    to_partner.wait()
+    project_near(near_rows)
+    attend(q, [(kb, vb)], att, (scores_a, scores_b), (peak_a, peak_b), (sums, tops), False)
+
+    @pl.when(has_other)
     def _():
-        to_next.wait_send()
-
-    @pl.when(me > 0)
+        to_other.wait()
+
+    @pl.when(jnp.logical_not(has_other))
     def _():
-        to_last.wait_send()
+        far_rows[...] = near_rows[...]
+
+    project_near(far_rows)
+    attend(q, [(kb, vb)], att, (scores_a, scores_b), (peak_a, peak_b), (sums, tops), True)
 
     @pl.loop(1, n)
     def _(offset):
@@ -253,6 +256,7 @@
     obs_operator, obs_owner, obs_row, obs_value,
 ):
     n = lax.axis_size("tm")
+    assert n % 2 == 0
     tokens = state[0]
     token_count, width = tokens.shape
     obs_count, channels = obs_value.shape
@@ -261,7 +265,7 @@
     rows = pltpu.VMEM((token_count, width), jnp.bfloat16)
     square = pltpu.VMEM((width, width), jnp.bfloat16)
     box = pltpu.VMEM((n, CAP, channels + LANES), jnp.bfloat16)
-    scores = pltpu.VMEM((2 * token_count, token_count), jnp.float32)
+    scores = pltpu.VMEM((token_count, token_count), jnp.float32)
     peak = pltpu.VMEM((8, token_count), jnp.float32)
     out = jax.ShapeDtypeStruct((token_count, width), jnp.bfloat16)
     drift, updated = pl.pallas_call(
@@ -270,9 +274,11 @@
         out_shape=(out, out),
         in_specs=[hbm, hbm, vmem, vmem] + [hbm] * 8 + [vmem] * 4,
         out_specs=(vmem, vmem),
-        scratch_shapes=[rows, rows] + [square] * 8 + [rows] * 12 + [
+        scratch_shapes=[rows, rows] + [square] * 8 + [rows] * 10 + [
             box, box,
             scores, scores, peak, peak,
+            pltpu.VMEM((HEADS, width // HEADS + 16, token_count), jnp.float32),
+            pltpu.VMEM((HEADS, 8, token_count), jnp.float32),
             pltpu.SemaphoreType.DMA((10,)),
             pltpu.SemaphoreType.DMA((2,)),
             pltpu.SemaphoreType.DMA((2,)),

time: 39.8 us -> 35.7 us (0.90)
  the two profiles are of different devices: /device:TPU:4 before, /device:TPU:0 now
where the time goes in v3:
time: 35.7 us; the launch traced here: 35.5 us
  Pallas kernels  32.1 us (90%)
  local copies, waits for them, and re-layouts  2.72 us (8%)
  between operations  0.65 us (2%)
    pallas_call x1, Pallas kernels, per_device(): pl.pallas_call(functools.partial(kernel, n), name='langevin', out_shape=(...  32.1 us
    unnamed x4, local copies, waits for them, and re-layouts  2.72 us

profile of v3, /device:TPU:0, one launch (start us, length us, event | category | flops | bytes accessed | tf_op | source)
XLA Modules:
  0.0 35.5 jit_solution(1484190907435001174)
XLA Ops:
  0.6 32.1 %langevin.1 = (bf16[512,512]{1,0:T(8,128)(2,1)}, bf16[512,512]{1,0:T(8,128)(2,1)}) custom-call(bf16[512,512]{1,0:T(8,128)(2,1)} %bitcast.8, bf16[512,512]{1,0:T(8,128)(2,1)} %bitcast.9, f32[1,512]{1,0:T(1,128)} %bitcast.12, f32[1,512]{1,0:T(1,128)} %bitcast.13, bf16[512,512]{1,0:T(8,128)(2,1)} %wq_hbm.1, bf16[512,512]{1,0:T(8,128)(2,1)} %wk_hbm.1, ...), custom_call_target="tpu_custom_call" | custom-call | tf_op jit(solution)/shard_map/langevin/pallas_call | solution.py:271
  32.8 0.0 copy-start
  32.8 1.9 %copy.20 = bf16[1,512,512]{2,1,0:T(8,128)(2,1)} copy(bf16[1,512,512]{2,1,0:T(8,128)(2,1)} %bitcast.11) | data formatting | bytes 1048576
  34.7 0.0 copy-done
  34.7 0.8 %copy.21 = bf16[1,512,512]{2,1,0:T(8,128)(2,1)} copy(bf16[1,512,512]{2,1,0:T(8,128)(2,1)S(1)} %bitcast.10) | data formatting | bytes 1048576
Async XLA Ops:
  32.8 1.9 %copy-start = (bf16[512,512]{1,0:T(8,128)(2,1)S(1)}, bf16[512,512]{1,0:T(8,128)(2,1)}, u32[]{:S(2)}) copy-start(bf16[512,512]{1,0:T(8,128)(2,1)} %get-tuple-element.5) | copy-start | bytes 1572868
